TPU v7x, 32 devices: a whole 2x2x4 slice. The times are simulated.
32 devices in a mesh: groups: 2 (over y), stripe: 8 (over z, x), exp: 2 (over core).
Axes of the slice: x: 2, y: 2, z: 4, core: 2. Of those that a mesh axis runs over, the one named last changes fastest.
Arguments:
- template: float32 [256, 2048], P(('groups', 'stripe'), 'exp'), parts along dimension 0, may hold values from -6 to 6
- exposure: float32 [4, 128, 2048], P(('groups', 'exp'), 'stripe'), parts along dimension 0, may hold values from -30 to 30
- cosmic_mask: int32 [4, 128, 2048], P(('groups', 'exp'), 'stripe'), parts along dimension 0, may hold values 0 or 1
- stamp_blocks: int32 [16, 16], P(('groups', 'stripe')), parts along dimension 0, may hold values from 0 to 31, as said below
- row_filters: float32 [19, 19], replicated, may hold values from -1 to 2.5
- col_filters: float32 [19, 19], replicated, may hold values from -1 to 2.5
Outputs:
- filtered: float32 [4, 128, 2048], P(('groups', 'exp'), 'stripe'), parts along dimension 0
- coefficients: float32 [4, 64], P(('groups', 'exp')), parts along dimension 0
There are 2 independent parts, one for each index of `groups`. A program takes and returns all parts, laid end to end along the dimension named above; an argument that names none is the same for every part. Nothing has to cross between parts.
Inputs may be any that keep to these rules, and one draw needn't show every extreme that they name: `stamp_blocks`: each row lists the stamps of one stripe; stamp j lies in column block 2 j or 2 j + 1.
All inputs are finite; a program needn't handle non-finite values. No bound on the sum of `cosmic_mask` on one device may be relied on, other than what follows from the above.
Results may differ from a plain program's by a relative error of at most 0.0003.
Values sent between devices are 32-bit elements; how exact they have to be, the bound alone decides.
A program may use at most 64 MiB of HBM per device.

v0:
```python
import functools

import jax
import jax.numpy as jnp
from jax import lax
from jax.experimental import pallas as pl
from jax.experimental.pallas import tpu as pltpu
from jax.sharding import PartitionSpec as P

HALF = 9
STAMP_W = 64
EDGE = 128
TILE = 8
BLOCK = 8
HIGHEST = lax.Precision.HIGHEST
MESH = pl.DeviceIdType.MESH


def round_up(n, m):
    return -(-n // m) * m


def row_coords(first, count, region_rows):
    index = lax.broadcasted_iota(jnp.int32, (count, 1), 0).astype(jnp.float32) + first
    return (2.0 * index + 1.0) / region_rows - 1.0


def col_coords(first, count, col_total):
    index = lax.broadcasted_iota(jnp.int32, (1, count), 1).astype(jnp.float32) + first
    return (2.0 * index + 1.0) / col_total - 1.0


def background(u, v):
    uu = 0.5 * (3.0 * u * u - 1.0)
    vv = 0.5 * (3.0 * v * v - 1.0)
    return [None, u, v, u * v, uu, vv, u * vv]


def split(x):
    high = x.astype(jnp.bfloat16)
    return high, (x - high.astype(jnp.float32)).astype(jnp.bfloat16)


def shifted_rows(row, count, start):
    return pltpu.roll(jnp.broadcast_to(row, (count, EDGE)), start, 1, stride=1, stride_axis=0)


def normal_kernel(region_rows, ext_ref, exp_ref, mask_ref, blk_ref, rowf_ref, colf_ref, out_ref, bandw, vert, design):
    bases, taps = rowf_ref.shape
    rows, cols = exp_ref.shape
    ext_rows = ext_ref.shape[0]
    fit = 3 * bases + 7
    total = out_ref.shape[0]
    half_cols = cols // 2
    blocks = half_cols // EDGE
    stamps = 2 * blocks
    low = lax.broadcasted_iota(jnp.int32, (1, EDGE), 1) < STAMP_W
    parity = [blk_ref[0, s] % 2 == 1 for s in range(stamps)]
    lanes = jnp.zeros((1, EDGE - taps), jnp.float32)

    windows = []
    for s in range(stamps):
        part = ext_ref[:, s * EDGE : (s + 3) * EDGE]
        early = pltpu.roll(part, 2 * EDGE + HALF, 1)[:, :EDGE]
        late = pltpu.roll(part, 2 * EDGE + HALF - STAMP_W, 1)[:, :EDGE]
        windows.append(jnp.where(parity[s], late, early))
    window = jnp.concatenate(windows, axis=1)
    w_high, w_rest = split(window)
    gap = jnp.zeros((EDGE - 2 * ext_rows, window.shape[1]), jnp.bfloat16)
    gap2 = jnp.zeros((EDGE - ext_rows, window.shape[1]), jnp.bfloat16)
    stacked = jnp.concatenate([w_high, w_rest, gap, w_high, gap2], axis=0)
    start = ext_rows // 2 - rows // 2 - HALF
    for b in range(bases):
        row = jnp.concatenate([rowf_ref[b : b + 1, :], lanes], axis=1)
        high = row.astype(jnp.bfloat16).astype(jnp.float32)
        twice = shifted_rows(high, rows, start) + shifted_rows(high, rows, start + ext_rows)
        rest = shifted_rows(row - high, rows, start)
        bandw[b * rows : (b + 1) * rows, :] = jnp.concatenate([twice, rest], axis=1)
    vert[...] = jnp.dot(bandw[...].astype(jnp.bfloat16), stacked, preferred_element_type=jnp.float32)

    def pick(x):
        parts = []
        for m in range(blocks):
            a = x[:, 2 * m * EDGE : (2 * m + 1) * EDGE]
            b = x[:, (2 * m + 1) * EDGE : (2 * m + 2) * EDGE]
            a = jnp.where(parity[2 * m], pltpu.roll(a, STAMP_W, 1), a)
            b = jnp.where(parity[2 * m + 1], b, pltpu.roll(b, STAMP_W, 1))
            parts.append(jnp.where(low, a, b))
        return jnp.concatenate(parts, axis=1)

    first = (lax.axis_index("stripe") * rows).astype(jnp.float32)
    v = jnp.broadcast_to(row_coords(first, rows, region_rows), (rows, half_cols))
    u_all = jnp.broadcast_to(col_coords(0.0, cols, cols), (8, cols))
    u = jnp.broadcast_to(pick(u_all)[0:1], (rows, half_cols))
    good = pick(mask_ref[...].astype(jnp.float32))

    def put(n, x):
        x = x * good
        for m in range(blocks):
            design[m, n * rows : (n + 1) * rows, :] = x[:, m * EDGE : (m + 1) * EDGE]

    for b in range(bases):
        x = vert[b * rows : (b + 1) * rows, :]
        x = jnp.concatenate([x[:, s * EDGE : (s + 1) * EDGE] for s in range(stamps)], axis=0)
        x_high, x_rest = split(x)
        row = jnp.concatenate([colf_ref[b : b + 1, :], lanes], axis=1)
        t_high, t_rest = split(shifted_rows(row, STAMP_W, 0))
        upper = jnp.concatenate([t_high, t_high], axis=1)
        lower = jnp.concatenate([t_rest, jnp.zeros_like(t_rest)], axis=1)
        y = lax.dot_general(
            jnp.concatenate([x_high, x_rest], axis=1),
            jnp.concatenate([upper, lower], axis=0),
            (((1,), (1,)), ((), ())),
            preferred_element_type=jnp.float32,
        )
        y = y + pltpu.roll(y, STAMP_W, 1)
        picked = jnp.concatenate(
            [
                jnp.where(low, y[2 * m * rows : (2 * m + 1) * rows], y[(2 * m + 1) * rows : (2 * m + 2) * rows])
                for m in range(blocks)
            ],
            axis=1,
        )
        put(3 * b, picked)
        put(3 * b + 1, picked * u)
        put(3 * b + 2, picked * v)

    terms = background(u, v)
    terms[0] = jnp.ones_like(u)
    for m, term in enumerate(terms):
        put(3 * bases + m, term)
    put(fit, pick(exp_ref[...]))
    for n in range(fit + 1, total):
        put(n, jnp.zeros_like(u))
    acc = jnp.zeros((total, total), jnp.float32)
    for r in range(rows):
        x = [design[m, pl.ds(r, total, stride=rows), :] for m in range(blocks)]
        x = jnp.concatenate(x, axis=1).astype(jnp.bfloat16)
        acc = acc + lax.dot_general(x, x, (((1,), (1,)), ((), ())), preferred_element_type=jnp.float32)
    out_ref[...] = jnp.concatenate([acc, jnp.zeros((total, EDGE - total), jnp.float32)], axis=1)


def exchange_halo(count, partners, tmpl_ref, exp_ref, mask_ref, ext_ref, edge_ref, parts, whole, extra_send, extra_recv, edge_send, edge_recv, send_sem, recv_sem):
    me = lax.axis_index("stripe")
    core = lax.axis_index("exp")
    rows, half = tmpl_ref.shape
    has_up = me > 0
    has_down = me < count - 1

    def copy(src, dst, n, stripe, exp):
        return pltpu.make_async_remote_copy(
            src_ref=src,
            dst_ref=dst,
            send_sem=send_sem.at[n],
            recv_sem=recv_sem.at[n],
            device_id={"stripe": stripe, "exp": exp},
            device_id_type=MESH,
        )

    def sends(way, stripe, tile):
        base = 5 * way
        return [
            copy(edge_send.at[way], edge_recv.at[way], base, stripe, core),
            copy(extra_send.at[way], extra_recv.at[2 * way], base + 1, stripe, core),
            copy(extra_send.at[way], extra_recv.at[2 * way + 1], base + 2, stripe, 1 - core),
            copy(tile, parts.at[2 * way], base + 3, stripe, core),
            copy(tile, parts.at[2 * way + 1], base + 4, stripe, 1 - core),
        ]

    def downs():
        return sends(0, me + 1, tmpl_ref.at[rows - TILE : rows])

    def ups():
        return sends(1, me - 1, tmpl_ref.at[0:TILE])

    more = HALF + 1 - TILE
    extra_send[0] = tmpl_ref[rows - TILE - more : rows - TILE, :]
    extra_send[1] = tmpl_ref[TILE : TILE + more, :]
    edge_send[0, 0:1, :] = exp_ref[rows - 1 : rows, :]
    edge_send[0, 1:2, :] = mask_ref[rows - 1 : rows, :].astype(jnp.float32)
    edge_send[1, 0:1, :] = exp_ref[0:1, :]
    edge_send[1, 1:2, :] = mask_ref[0:1, :].astype(jnp.float32)
    barrier = pltpu.get_barrier_semaphore()

    def greet(stripe, exp):
        pl.semaphore_signal(barrier, inc=1, device_id={"stripe": stripe, "exp": exp}, device_id_type=MESH)

    @pl.when(has_up)
    def _():
        greet(me - 1, core)
        greet(me - 1, 1 - core)

    @pl.when(has_down)
    def _():
        greet(me + 1, core)
        greet(me + 1, 1 - core)

    greet(me, 1 - core)
    for partner in partners:
        greet(partner, core)
    pl.semaphore_wait(barrier, 1 + len(partners) + 2 * has_up.astype(jnp.int32) + 2 * has_down.astype(jnp.int32))

    @pl.when(has_down)
    def _():
        for c in downs()[::-1]:
            c.start()

    @pl.when(has_up)
    def _():
        for c in ups()[::-1]:
            c.start()

    across = copy(tmpl_ref, whole, 10, me, 1 - core)
    across.start()
    ext_ref[...] = jnp.zeros_like(ext_ref)
    edge_ref[...] = jnp.zeros_like(edge_ref)
    mine = pl.ds(pl.multiple_of(EDGE + core * half, EDGE), half)
    theirs = pl.ds(pl.multiple_of(EDGE + (1 - core) * half, EDGE), half)
    ext_ref[rows : 2 * rows, mine] = tmpl_ref[...]
    across.wait()
    ext_ref[rows : 2 * rows, theirs] = whole[...]

    @pl.when(has_up)
    def _():
        for c in downs()[1:]:
            c.wait_recv()
        for n, lanes in enumerate((mine, theirs)):
            ext_ref[rows - TILE : rows, lanes] = parts[n]
            ext_ref[rows - TILE - more : rows - TILE, lanes] = extra_recv[n]

    @pl.when(has_down)
    def _():
        for c in ups()[1:]:
            c.wait_recv()
        for n, lanes in enumerate((mine, theirs)):
            ext_ref[2 * rows : 2 * rows + TILE, lanes] = parts[2 + n]
            ext_ref[2 * rows + TILE : 2 * rows + TILE + more, lanes] = extra_recv[2 + n]

    def finish():
        @pl.when(has_up)
        def _():
            downs()[0].wait_recv()
            edge_ref[0] = edge_recv[0]
            for c in ups():
                c.wait_send()

        @pl.when(has_down)
        def _():
            ups()[0].wait_recv()
            edge_ref[1] = edge_recv[1]
            for c in downs():
                c.wait_send()

    return finish


def fit_kernel(
    count,
    fit,
    region_rows,
    tmpl_ref,
    exp_ref,
    mask_ref,
    blk_ref,
    rowf_ref,
    colf_ref,
    out_ref,
    ext_ref,
    edge_ref,
    parts,
    whole,
    extra_send,
    extra_recv,
    edge_send,
    edge_recv,
    halo_send,
    halo_recv,
    local_ref,
    bandw,
    vert,
    design,
    send,
    held,
    send_sem,
    recv_sem,
):
    me = lax.axis_index("stripe")
    steps = []
    d = 1
    while d < count:
        steps.append(d)
        d *= 2
    partners = [me + d * (1 - 2 * ((me // d) % 2)) for d in steps]
    finish = exchange_halo(
        count,
        partners,
        tmpl_ref,
        exp_ref,
        mask_ref,
        ext_ref,
        edge_ref,
        parts,
        whole,
        extra_send,
        extra_recv,
        edge_send,
        edge_recv,
        halo_send,
        halo_recv,
    )
    normal_kernel(
        region_rows, ext_ref, exp_ref, mask_ref, blk_ref, rowf_ref, colf_ref, local_ref, bandw, vert, design
    )
    total = local_ref[...]
    for s, partner in enumerate(partners):
        source = local_ref
        if s:
            send[s] = total
            source = send.at[s]
        copy = pltpu.make_async_remote_copy(
            src_ref=source,
            dst_ref=held.at[s],
            send_sem=send_sem.at[s],
            recv_sem=recv_sem.at[s],
            device_id={"stripe": partner},
            device_id_type=MESH,
        )
        copy.start()
        copy.wait()
        total = total + held[s]
    a = total[:fit, :]
    sub = lax.broadcasted_iota(jnp.int32, a.shape, 0)
    for first in range(0, fit, BLOCK):
        block = range(first, min(first + BLOCK, fit))
        cols = [jnp.broadcast_to(a[:, k : k + 1], a.shape) for k in block]
        for t, k in enumerate(block):
            inverse = pl.reciprocal(cols[t][k : k + 1, :])
            row = a[k : k + 1, :] * inverse
            a = jnp.where(sub == k, row, a - cols[t] * row)
            for w in range(t + 1, len(block)):
                factor = cols[w][k : k + 1, :] * inverse
                cols[w] = jnp.where(sub == k, factor, cols[w] - cols[t] * factor)
    answer = jnp.broadcast_to(a[:, fit : fit + 1], a.shape)
    out_ref[...] = jnp.zeros_like(out_ref)
    out_ref[:fit, :] = answer
    finish()


def model_kernel(region_rows, coef_ref, ext_ref, exp_ref, mask_ref, edge_ref, rowf_ref, colf_ref, out_ref, row_ref, band, wide_y, diff):
    rows, cols = out_ref.shape
    bases, taps = rowf_ref.shape
    fit = 3 * bases + 7
    tall = diff.shape[0]
    answer = coef_ref[:fit, :fit]
    same = lax.broadcasted_iota(jnp.int32, (fit, fit), 0) == lax.broadcasted_iota(jnp.int32, (fit, fit), 1)
    row_ref[...] = jnp.sum(jnp.where(same, answer, 0.0), axis=0, keepdims=True)
    ext_rows, wide = ext_ref.shape
    first = (lax.axis_index("stripe") * rows - 1).astype(jnp.float32)
    v = row_coords(first, tall, region_rows)
    rowf = jnp.concatenate([rowf_ref[...], jnp.zeros((bases, EDGE - taps), jnp.float32)], axis=1)
    colf = jnp.concatenate([colf_ref[...], jnp.zeros((bases, EDGE - taps), jnp.float32)], axis=1)
    start = ext_rows // 2 - rows // 2 - HALF - 1
    mats = []
    for t in range(3):
        c = coef_ref[pl.ds(t, bases, stride=3), :]
        mats.append(
            lax.dot_general(
                colf * c,
                rowf,
                (((0,), (0,)), ((), ())),
                precision=HIGHEST,
                preferred_element_type=jnp.float32,
            )
        )
    for j in range(taps):
        k0, k1, k2 = (jnp.broadcast_to(m[j : j + 1, :], (tall, EDGE)) for m in mats)
        main = k0 + v * k2 + (-(j - HALF) * 2.0 / cols) * k1
        main = shifted_rows(main, tall, start)
        side = shifted_rows(k1, tall, start + ext_rows)
        band[j * tall : (j + 1) * tall, :] = main + side
    ext = ext_ref[...]
    u_wide = col_coords(-float(EDGE), wide, cols)
    both = jnp.concatenate([ext, ext * u_wide, jnp.zeros((EDGE - 2 * ext_rows, wide), jnp.float32)], axis=0)
    high, rest = split(both)
    w_high, w_rest = split(band[...])
    dot = functools.partial(jnp.dot, preferred_element_type=jnp.float32)
    wide_y[...] = dot(w_high, high) + (dot(w_high, rest) + dot(w_rest, high))
    u = col_coords(0.0, cols, cols)
    q = [coef_ref[3 * bases + m : 3 * bases + m + 1, 0:1] for m in range(7)]
    terms = background(u, v)
    level = q[0] + q[1] * terms[1] + q[4] * terms[4]
    model = level + (q[2] * terms[2] + q[5] * terms[5]) + u * (q[3] * v + q[6] * terms[5])
    for j in range(taps):
        y = wide_y[j * tall : (j + 1) * tall, :]
        model = model + pltpu.roll(y, wide - (EDGE - HALF) - j, 1)[:, :cols]
    spare = jnp.zeros((tall - rows - 2, cols), jnp.float32)
    science = jnp.concatenate([edge_ref[0, 0:1, :], exp_ref[...], edge_ref[1, 0:1, :], spare], axis=0)
    good = jnp.concatenate(
        [edge_ref[0, 1:2, :], mask_ref[...].astype(jnp.float32), edge_ref[1, 1:2, :], spare], axis=0
    )
    diff[...] = good * (science - model)
    lane = lax.broadcasted_iota(jnp.int32, (rows, cols), 1)
    mid = diff[1 : rows + 1, :]
    left = jnp.where(lane == 0, 0.0, pltpu.roll(mid, 1, 1))
    right = jnp.where(lane == cols - 1, 0.0, pltpu.roll(mid, cols - 1, 1))
    around = diff[2 : rows + 2, :] + diff[0:rows, :] + right + left
    out_ref[...] = 4.0 * mid - around


def shards(template, exposure, cosmic_mask, stamp_blocks, row_filters, col_filters):
    rows, cols = exposure.shape[1:]
    bases, taps = row_filters.shape
    fit = 3 * bases + 7
    stripes = lax.axis_size("stripe")
    region_rows = rows * stripes
    own_exp = exposure[0]
    own_mask = cosmic_mask[0]
    half = template.shape[1]
    ext_rows = 3 * rows
    wide = cols + 2 * EDGE
    tall = round_up(rows + 2, 8)
    total = round_up(fit + 1, 8)
    vmem = pl.BlockSpec(memory_space=pltpu.VMEM)
    smem = pl.BlockSpec(memory_space=pltpu.SMEM)
    f32 = jnp.float32
    hops = max(1, (stripes - 1).bit_length())
    coef, ext, edges = pl.pallas_call(
        functools.partial(fit_kernel, stripes, fit, float(region_rows)),
        out_shape=(
            jax.ShapeDtypeStruct((total, EDGE), f32),
            jax.ShapeDtypeStruct((ext_rows, wide), f32),
            jax.ShapeDtypeStruct((2, 2, cols), f32),
        ),
        in_specs=[vmem] * 3 + [smem] + [vmem] * 2,
        out_specs=(vmem, vmem, vmem),
        scratch_shapes=[
            pltpu.VMEM((4, TILE, half), f32),
            pltpu.VMEM((rows, half), f32),
            pltpu.VMEM((2, HALF + 1 - TILE, half), f32),
            pltpu.VMEM((4, HALF + 1 - TILE, half), f32),
            pltpu.VMEM((2, 2, cols), f32),
            pltpu.VMEM((2, 2, cols), f32),
            pltpu.SemaphoreType.DMA((11,)),
            pltpu.SemaphoreType.DMA((11,)),
            pltpu.VMEM((total, EDGE), f32),
            pltpu.VMEM((bases * rows, 2 * EDGE), f32),
            pltpu.VMEM((bases * rows, cols), f32),
            pltpu.VMEM((cols // (2 * EDGE), total * rows, EDGE), f32),
            pltpu.VMEM((hops, total, EDGE), f32),
            pltpu.VMEM((hops, total, EDGE), f32),
            pltpu.SemaphoreType.DMA((hops,)),
            pltpu.SemaphoreType.DMA((hops,)),
        ],
        compiler_params=pltpu.CompilerParams(collective_id=0, has_side_effects=True),
        name="fit",
    )(template, own_exp, own_mask, stamp_blocks, row_filters, col_filters)
    filtered, coef_row = pl.pallas_call(
        functools.partial(model_kernel, float(region_rows)),
        out_shape=(jax.ShapeDtypeStruct((rows, cols), f32), jax.ShapeDtypeStruct((1, fit), f32)),
        in_specs=[vmem] * 7,
        out_specs=(vmem, vmem),
        scratch_shapes=[
            pltpu.VMEM((taps * tall, EDGE), f32),
            pltpu.VMEM((taps * tall, wide), f32),
            pltpu.VMEM((tall, cols), f32),
        ],
        name="model",
    )(coef, ext, own_exp, own_mask, edges, row_filters, col_filters)
    return (filtered[None], coef_row)


def solution(mesh):
    placed = (
        P(("groups", "stripe"), "exp"),
        P(("groups", "exp"), "stripe", None),
        P(("groups", "exp"), "stripe", None),
        P(("groups", "stripe"), None),
        P(),
        P(),
    )
    return jax.shard_map(
        shards,
        mesh=mesh,
        in_specs=placed,
        out_specs=(P(("groups", "exp"), "stripe", None), P(("groups", "exp"), None)),
        check_vma=False,
    )
```

profile of v0, /device:TPU:0, one launch (start us, length us, event | category | flops | bytes accessed | tf_op | source)
XLA Modules:
  0.0 31.9 jit_solution(12089512219509834087)
XLA Ops:
  0.6 26.5 %fit.1 = (f32[72,128]{1,0:T(8,128)}, f32[48,2304]{1,0:T(8,128)}, f32[2,2,2048]{2,1,0:T(2,128)}) custom-call(f32[16,1024]{1,0:T(8,128)} %tmpl_ref.1, f32[16,2048]{1,0:T(8,128)} %bitcast.3, s32[16,2048]{1,0:T(8,128)} %bitcast.5, s32[1,16]{1,0:T(1,128)} %blk_ref.1, f32[19,19]{1,0:T(8,128)} %rowf_ref.3, f32[19,19]{1,0:T(8,128)} %colf_ref.3), custom_call_target="tpu_custom_call" | custom-call | tf_op jit(solution)/shard_map/fit/pallas_call | solution.py:427
  27.2 4.8 %model.1 = (f32[16,2048]{1,0:T(8,128)}, f32[1,64]{1,0:T(1,128)}) custom-call(f32[72,128]{1,0:T(8,128)} %get-tuple-element.7.coef_ref, f32[48,2304]{1,0:T(8,128)} %get-tuple-element.8.ext_ref, f32[16,2048]{1,0:T(8,128)} %bitcast.4, s32[16,2048]{1,0:T(8,128)} %bitcast.6, f32[2,2,2048]{2,1,0:T(2,128)} %get-tuple-element.9.edge_ref, f32[19,19]{1,0:T(8,128)} %rowf_ref.3, ...), custom_call_target="tpu_custom_call" | custom-call | tf_op jit(solution)/shard_map/model/pallas_call | solution.py:457
where the time goes:
time: 32.1 us; the launch traced here: 31.9 us
  Pallas kernels  31.3 us (98%)
  between operations  0.64 us (2%)
    pallas_call x1, Pallas kernels, shards(): pl.pallas_call(functools.partial(fit_kernel, stripes, fit, float(region_r...  26.5 us
    pallas_call x1, Pallas kernels, shards(): pl.pallas_call(functools.partial(model_kernel, float(region_rows)), out_s...  4.77 us

commit v1 on v0

v1 whole, which is shorter than its diff:
```python
import functools

import jax
import jax.numpy as jnp
from jax import lax
from jax.experimental import pallas as pl
from jax.experimental.pallas import tpu as pltpu
from jax.sharding import PartitionSpec as P

HALF = 9
STAMP_W = 64
EDGE = 128
TILE = 8
BLOCK = 8
REACH = HALF + 1
MESH = pl.DeviceIdType.MESH
LANE_DOT = (((1,), (1,)), ((), ()))


def round_up(n, m):
    return -(-n // m) * m


def row_coords(index, region_rows):
    return (2.0 * index + 1.0) / region_rows - 1.0


def col_coords(first, count, col_total):
    index = lax.broadcasted_iota(jnp.int32, (1, count), 1).astype(jnp.float32) + first
    return (2.0 * index + 1.0) / col_total - 1.0


def background(u, v):
    uu = 0.5 * (3.0 * u * u - 1.0)
    vv = 0.5 * (3.0 * v * v - 1.0)
    return [None, u, v, u * v, uu, vv, u * vv]


def split(x):
    high = x.astype(jnp.bfloat16)
    return high, (x - high.astype(jnp.float32)).astype(jnp.bfloat16)


def shifted_rows(row, count, start):
    return pltpu.roll(jnp.broadcast_to(row, (count, EDGE)), start, 1, stride=1, stride_axis=0)


def iotas(rows):
    return lax.broadcasted_iota(jnp.int32, (rows, EDGE), 0), lax.broadcasted_iota(jnp.int32, (rows, EDGE), 1)


def turn(x, shift, axis):
    return pltpu.roll(x, shift % x.shape[axis], axis)


def squeeze_terms(a, bases, axis):
    padded = round_up(bases, TILE)
    gap = padded - bases
    index = lax.broadcasted_iota(jnp.int32, a.shape, axis)
    out = a
    for t in range(1, 4):
        out = jnp.where(index >= t * bases, turn(a, -t * gap, axis), out)
    return out


def pack_normal(gram, fit):
    half = fit // 2
    rows = gram.shape[0]
    sub, lane = iotas(half)
    one = lane[0:1]
    upper, lower = gram[:half], gram[half:fit]
    merged = jnp.where((lane > sub) & (lane < half), turn(lower, -half, 1), upper)
    fold = half // 2
    body = jnp.where(lane[:fold] < fit, merged[:fold], turn(merged[fold:], fit, 1))
    diag = jnp.sum(jnp.where(lane == sub + half, lower, 0.0), axis=0, keepdims=True)
    last = jnp.where(one < fit, gram[fit : fit + 1], jnp.where(one < fit + half, turn(diag, half, 1), 0.0))
    return body, last


def unpack_normal(body, last, fit):
    half = fit // 2
    sub, lane = iotas(half)
    quad = jnp.concatenate([body, turn(body, fit, 1)], axis=0)
    tall = jnp.concatenate([quad, jnp.broadcast_to(last, (TILE, EDGE))], axis=0)
    flip = jnp.transpose(tall, (1, 0))[:fit]
    flip = jnp.concatenate([flip, jnp.zeros((fit, EDGE - flip.shape[1]), jnp.float32)], axis=1)
    side = turn(flip, half, 1)
    first, second = flip[:half], flip[half:]
    diag = jnp.broadcast_to(turn(last, -fit, 1), (half, EDGE))
    top = jnp.where(lane < half, jnp.where(lane <= sub, quad, first), jnp.where(lane < fit, quad, side[:half]))
    corner = jnp.where(lane > sub, quad, jnp.where(lane == sub, diag, first))
    low = jnp.where(lane < half, second, jnp.where(lane < fit, turn(corner, half, 1), side[half:]))
    return jnp.concatenate([top, low], axis=0)


def eliminate(a, fit):
    sub = lax.broadcasted_iota(jnp.int32, a.shape, 0)
    for first in range(0, fit, BLOCK):
        block = range(first, min(first + BLOCK, fit))
        cols = [jnp.broadcast_to(a[:, k : k + 1], a.shape) for k in block]
        for t, k in enumerate(block):
            inverse = pl.reciprocal(cols[t][k : k + 1, :])
            row = a[k : k + 1, :] * inverse
            a = jnp.where(sub == k, row, a - cols[t] * row)
            for w in range(t + 1, len(block)):
                factor = cols[w][k : k + 1, :] * inverse
                cols[w] = jnp.where(sub == k, factor, cols[w] - cols[t] * factor)
    return jnp.broadcast_to(a[:, fit : fit + 1], a.shape)


def kernel(
    count,
    region_rows,
    radices,
    rounds,
    tmpl_hbm,
    exp_hbm,
    mask_hbm,
    blk_hbm,
    rowf_hbm,
    colf_hbm,
    out_ref,
    row_ref,
    tmpl_ref,
    exp_ref,
    mask_ref,
    blk_ref,
    rowf_ref,
    colf_ref,
    halo_send,
    halo_own,
    halo_other,
    whole,
    edge_send,
    edge_recv,
    ext_ref,
    bandw,
    bandf,
    toep_s,
    toep_f,
    vert,
    design,
    ground,
    vert_f,
    basis,
    coef_ref,
    plane,
    diff,
    send,
    held,
    load_sem,
    halo_ss,
    halo_rs,
    red_ss,
    red_rs,
    hello,
):
    me = lax.axis_index("stripe")
    core = lax.axis_index("exp")
    rows, half = tmpl_ref.shape
    cols = exp_ref.shape[1]
    bases, taps = rowf_ref.shape
    fit = 3 * bases + 7
    pad_b = round_up(bases, TILE)
    ext_rows, wide = ext_ref.shape
    tall = diff.shape[0]
    half_cols = cols // 2
    blocks = half_cols // EDGE
    stamps = 2 * blocks
    tiles = cols // EDGE
    has_up = me > 0
    has_down = me < count - 1
    up_count = has_up.astype(jnp.int32)
    down_count = has_down.astype(jnp.int32)

    barrier = pltpu.get_barrier_semaphore()

    def greet(sem, stripe, exp):
        pl.semaphore_signal(sem, inc=1, device_id={"stripe": stripe, "exp": exp}, device_id_type=MESH)

    @pl.when(has_up)
    def _():
        greet(barrier, me - 1, core)

    @pl.when(has_down)
    def _():
        greet(barrier, me + 1, core)

    greet(barrier, me, 1 - core)

    loads = [
        pltpu.make_async_copy(src, dst, load_sem.at[n])
        for n, (src, dst) in enumerate(
            (
                (tmpl_hbm, tmpl_ref),
                (exp_hbm, exp_ref),
                (mask_hbm, mask_ref),
                (blk_hbm, blk_ref),
                (rowf_hbm, rowf_ref),
                (colf_hbm, colf_ref),
            )
        )
    ]
    for c in loads:
        c.start()

    ext_ref[...] = jnp.zeros_like(ext_ref)

    @pl.when(jnp.logical_not(has_up))
    def _():
        halo_own[0] = jnp.zeros_like(halo_own[0])
        halo_other[0] = jnp.zeros_like(halo_other[0])
        edge_recv[0] = jnp.zeros_like(edge_recv[0])

    @pl.when(jnp.logical_not(has_down))
    def _():
        halo_own[1] = jnp.zeros_like(halo_own[1])
        halo_other[1] = jnp.zeros_like(halo_other[1])
        edge_recv[1] = jnp.zeros_like(edge_recv[1])

    def copy(src, dst, n, stripe, exp):
        return pltpu.make_async_remote_copy(
            src_ref=src,
            dst_ref=dst,
            send_sem=halo_ss.at[n],
            recv_sem=halo_rs.at[n],
            device_id={"stripe": stripe, "exp": exp},
            device_id_type=MESH,
        )

    def halo(way):
        return copy(halo_send.at[way], halo_own.at[way], way, me + 1 - 2 * way, core)

    def edge(way):
        return copy(edge_send.at[way], edge_recv.at[way], 2 + way, me + 1 - 2 * way, core)

    def relay(way):
        return copy(halo_own.at[way], halo_other.at[way], 4 + way, me, 1 - core)

    more = REACH - TILE
    for c in loads:
        c.wait()
    halo_send[0, 0:TILE] = tmpl_ref[rows - TILE : rows]
    halo_send[0, TILE:REACH] = tmpl_ref[rows - REACH : rows - TILE]
    halo_send[1] = tmpl_ref[0:REACH]
    edge_send[0, 0:1, :] = exp_ref[rows - 1 : rows, :]
    edge_send[0, 1:2, :] = mask_ref[rows - 1 : rows, :].astype(jnp.float32)
    edge_send[1, 0:1, :] = exp_ref[0:1, :]
    edge_send[1, 1:2, :] = mask_ref[0:1, :].astype(jnp.float32)

    pl.semaphore_wait(barrier, 1 + up_count + down_count)

    @pl.when(has_down)
    def _():
        halo(0).start()

    @pl.when(has_up)
    def _():
        halo(1).start()

    across = copy(tmpl_ref, whole, 6, me, 1 - core)
    across.start()

    @pl.when(has_down)
    def _():
        edge(0).start()

    @pl.when(has_up)
    def _():
        edge(1).start()

    def call(n):
        reach = 1 << n

        @pl.when(me >= reach)
        def _():
            greet(hello.at[n], me - reach, core)

        @pl.when(me + reach < count)
        def _():
            greet(hello.at[n], me + reach, core)

    def listen(n):
        reach = 1 << n
        heard = (me >= reach).astype(jnp.int32) + (me + reach < count).astype(jnp.int32)
        pl.semaphore_wait(hello.at[n], heard)

    if rounds:
        call(0)

    lanes = jnp.zeros((1, EDGE - taps), jnp.float32)
    low = lax.broadcasted_iota(jnp.int32, (1, EDGE), 1) < STAMP_W
    parity = [blk_ref[0, s] % 2 == 1 for s in range(stamps)]

    def pick(x):
        parts = []
        for m in range(blocks):
            a = x[:, 2 * m * EDGE : (2 * m + 1) * EDGE]
            b = x[:, (2 * m + 1) * EDGE : (2 * m + 2) * EDGE]
            a = jnp.where(parity[2 * m], pltpu.roll(a, STAMP_W, 1), a)
            b = jnp.where(parity[2 * m + 1], b, pltpu.roll(b, STAMP_W, 1))
            parts.append(jnp.where(low, a, b))
        return jnp.concatenate(parts, axis=1)

    start = ext_rows // 2 - rows // 2 - HALF
    sub_e, lane_e = iotas(EDGE)
    sub_t = lax.broadcasted_iota(jnp.int32, (TILE, EDGE), 0)
    for b in range(bases):
        row = jnp.concatenate([rowf_ref[b : b + 1, :], lanes], axis=1)
        high = row.astype(jnp.bfloat16).astype(jnp.float32)

        def placed(x, offset):
            body = shifted_rows(x, rows + TILE, start + offset)
            above = pltpu.roll(jnp.broadcast_to(x, (TILE, EDGE)), start + offset - 1, 1)
            tail = jnp.where(sub_t == TILE - 1, above, body[rows:])
            return body[:rows], jnp.concatenate([body[:rows], tail], axis=0)

        (h0, h0f), (h1, h1f), (r0, r0f) = placed(high, 0), placed(high, ext_rows), placed(row - high, 0)
        bandw[b * rows : (b + 1) * rows, :] = jnp.concatenate([h0 + h1, r0], axis=1)
        bandf[b * tall : (b + 1) * tall, :] = jnp.concatenate([h0f + h1f, r0f], axis=1)
        row = jnp.concatenate([colf_ref[b : b + 1, :], lanes], axis=1)
        spread = shifted_rows(row, EDGE, 0)
        t_high, t_rest = split(spread[:STAMP_W])
        upper = jnp.concatenate([t_high, t_high], axis=1)
        lower = jnp.concatenate([t_rest, jnp.zeros_like(t_rest)], axis=1)
        toep_s[b] = jnp.concatenate([upper, lower], axis=0)
        inside = jnp.where(lane_e >= sub_e, spread, 0.0)
        f_high, f_rest = split(jnp.concatenate([inside, spread - inside], axis=1))
        upper = jnp.concatenate([f_high, f_high], axis=1)
        lower = jnp.concatenate([f_rest, jnp.zeros_like(f_rest)], axis=1)
        toep_f[b] = jnp.concatenate([upper, lower], axis=0)

    first = (me * rows).astype(jnp.float32)
    index = lax.broadcasted_iota(jnp.int32, (rows, 1), 0).astype(jnp.float32)
    v = jnp.broadcast_to(row_coords(index + first, region_rows), (rows, half_cols))
    u_all = jnp.broadcast_to(col_coords(0.0, cols, cols), (TILE, cols))
    u_sel = pick(u_all)
    u = jnp.concatenate([u_sel] * (rows // TILE), axis=0)
    good = pick(mask_ref[...].astype(jnp.float32))
    terms = background(u, v)
    terms[0] = jnp.ones_like(u)
    terms.append(pick(exp_ref[...]))
    for k, term in enumerate(terms):
        x = term * good
        for m in range(blocks):
            ground[m, pl.ds(k, rows, stride=TILE), :] = x[:, m * EDGE : (m + 1) * EDGE]
    zero = jnp.zeros((rows, EDGE), jnp.float32)
    for b in range(bases, pad_b):
        for m in range(blocks):
            design[m, pl.ds(b, rows, stride=pad_b), :] = zero

    if rounds:
        listen(0)
    if rounds > 1:
        call(1)

    @pl.when(has_up)
    def _():
        halo(0).wait_recv()
        relay(0).start()

    @pl.when(has_down)
    def _():
        halo(1).wait_recv()
        relay(1).start()

    across.wait_recv()
    mine = pl.ds(pl.multiple_of(EDGE + core * half, EDGE), half)
    theirs = pl.ds(pl.multiple_of(EDGE + (1 - core) * half, EDGE), half)
    ext_ref[rows : 2 * rows, mine] = tmpl_ref[...]
    ext_ref[rows : 2 * rows, theirs] = whole[...]

    @pl.when(has_up)
    def _():
        relay(0).wait_recv()

    @pl.when(has_down)
    def _():
        relay(1).wait_recv()

    for n, (buf, where) in enumerate(((halo_own, mine), (halo_other, theirs))):
        ext_ref[rows - TILE : rows, where] = buf[0, 0:TILE]
        ext_ref[rows - REACH : rows - TILE, where] = buf[0, TILE:REACH]
        ext_ref[2 * rows : 2 * rows + REACH, where] = buf[1]
    ext = turn(ext_ref[...], -(EDGE - HALF), 1)
    ext_ref[...] = ext

    for n in range(1, rounds):
        listen(n)
        if n + 1 < rounds:
            call(n + 1)

    windows = []
    for s in range(stamps):
        early = ext[:, s * EDGE : (s + 1) * EDGE]
        after = ext[:, (s + 1) * EDGE : (s + 2) * EDGE]
        late = pltpu.roll(jnp.where(low, after, early), STAMP_W, 1)
        windows.append(jnp.where(parity[s], late, early))

    def stack(x):
        high, rest = split(x)
        gap = jnp.zeros((EDGE - 2 * ext_rows, x.shape[1]), jnp.bfloat16)
        gap2 = jnp.zeros((EDGE - ext_rows, x.shape[1]), jnp.bfloat16)
        return jnp.concatenate([high, rest, gap, high, gap2], axis=0)

    window = jnp.concatenate(windows, axis=1)
    vert[...] = jnp.dot(bandw[...].astype(jnp.bfloat16), stack(window), preferred_element_type=jnp.float32)

    for b in range(bases):
        x = vert[b * rows : (b + 1) * rows, :]
        x = jnp.concatenate([x[:, s * EDGE : (s + 1) * EDGE] for s in range(stamps)], axis=0)
        y = lax.dot_general(
            jnp.concatenate(split(x), axis=1), toep_s[b], LANE_DOT, preferred_element_type=jnp.float32
        )
        y = y + pltpu.roll(y, STAMP_W, 1)
        for m in range(blocks):
            picked = jnp.where(low, y[2 * m * rows : (2 * m + 1) * rows], y[(2 * m + 1) * rows : (2 * m + 2) * rows])
            design[m, pl.ds(b, rows, stride=pad_b), :] = picked * good[:, m * EDGE : (m + 1) * EDGE]

    total = 3 * pad_b + TILE
    acc = jnp.zeros((total, total), jnp.float32)
    for r in range(rows):
        parts = []
        for m in range(blocks):
            d = design[m, r * pad_b : (r + 1) * pad_b, :]
            um = u_sel[0:1, m * EDGE : (m + 1) * EDGE]
            vm = v[r : r + 1, 0:EDGE]
            parts.append(jnp.concatenate([d, d * um, d * vm, ground[m, r * TILE : (r + 1) * TILE, :]], axis=0))
        x = jnp.concatenate(parts, axis=1).astype(jnp.bfloat16)
        acc = acc + lax.dot_general(x, x, LANE_DOT, preferred_element_type=jnp.float32)
    gram = jnp.concatenate([acc, jnp.zeros((total, EDGE - total), jnp.float32)], axis=1)
    gram = squeeze_terms(squeeze_terms(gram, bases, 0), bases, 1)
    body, last = pack_normal(gram, fit)

    def reduce_start(phase, base, stride, radix):
        digit = (me // stride) % radix
        copies = []
        for k in range(radix - 1, 0, -1):
            other = digit * 0
            for bit in range((radix - 1).bit_length()):
                on = (digit // (1 << bit)) % 2
                other = other + ((1 - on) if (k >> bit) & 1 else on) * (1 << bit)
            copies.append(
                pltpu.make_async_remote_copy(
                    src_ref=send.at[phase],
                    dst_ref=held.at[base + k - 1],
                    send_sem=red_ss.at[base + k - 1],
                    recv_sem=red_rs.at[base + k - 1],
                    device_id={"stripe": me + (other - digit) * stride},
                    device_id_type=MESH,
                )
            )
        for c in copies:
            c.start()
        return copies

    fold = body.shape[0]

    def put(phase, parts):
        send[phase, 0:fold] = parts[0]
        send[phase, fold : fold + 1] = parts[1]

    def tree(values):
        while len(values) > 1:
            values = [values[q] + values[q + 1] for q in range(0, len(values), 2)]
        return values[0]

    base, stride, flying = 0, 1, []
    for phase, radix in enumerate(radices):
        put(phase, (body, last))
        copies = reduce_start(phase, base, stride, radix)
        flying += copies
        if phase == 0:
            vert_f[...] = jnp.dot(
                bandf[...].astype(jnp.bfloat16), stack(ext_ref[...]), preferred_element_type=jnp.float32
            )
            for b in range(bases):
                x = vert_f[b * tall : (b + 1) * tall, :]
                x = jnp.concatenate([x[:, m * EDGE : (m + 2) * EDGE] for m in range(tiles)], axis=0)
                y = lax.dot_general(
                    jnp.concatenate(split(x), axis=1), toep_f[b], LANE_DOT, preferred_element_type=jnp.float32
                )
                basis[b] = y[:, :EDGE] + y[:, EDGE:]
        for c in copies:
            c.wait_recv()
        body = tree([send[phase, 0:fold]] + [held[base + k, 0:fold] for k in range(radix - 1)])
        last = tree([send[phase, fold : fold + 1]] + [held[base + k, fold : fold + 1] for k in range(radix - 1)])
        base += radix - 1
        stride *= radix

    answer = eliminate(unpack_normal(body, last, fit), fit)
    coef_ref[...] = answer
    n = lax.broadcasted_iota(jnp.int32, (fit, fit), 0)
    term = (n >= bases).astype(jnp.int32) + (n >= 2 * bases).astype(jnp.int32)
    spot = jnp.where(n < 3 * bases, 3 * (n - bases * term) + term, n)
    same = spot == lax.broadcasted_iota(jnp.int32, (fit, fit), 1)
    row_ref[...] = jnp.sum(jnp.where(same, answer[:, :fit], 0.0), axis=0, keepdims=True)

    for c in (0, 1):
        @pl.when((has_up, has_down)[c])
        def _():
            edge(c).wait_recv()

    def coef(n):
        return coef_ref[pl.ds(n, TILE, stride=0), :]

    def three(x):
        return jnp.concatenate([x] * (tall // TILE), axis=0)

    place = lax.broadcasted_iota(jnp.int32, (tall, EDGE), 0)
    place = jnp.where(place == tall - 1, -1, place).astype(jnp.float32)
    v = row_coords(place + first, region_rows)
    vv = 0.5 * (3.0 * v * v - 1.0)
    for b in range(bases):
        plane[b, 0:tall] = three(coef(b)) + v * three(coef(2 * bases + b))
        plane[b, tall : tall + TILE] = coef(bases + b)
    q = [coef(3 * bases + k) for k in range(7)]
    flat = three(q[0]) + v * three(q[2]) + vv * three(q[5])
    slope = three(q[1]) + v * three(q[3]) + vv * three(q[6])
    u_all = col_coords(0.0, cols, cols)
    spare = jnp.zeros((tall - rows - 2, EDGE), jnp.float32)
    for m in range(tiles):
        at = slice(m * EDGE, (m + 1) * EDGE)
        um = jnp.broadcast_to(u_all[:, at], (TILE, EDGE))
        uu = 0.5 * (3.0 * um * um - 1.0)
        model = flat + three(um) * slope + three(q[4] * uu)
        for b in range(bases):
            factor = plane[b, 0:tall] + three(um * plane[b, tall : tall + TILE])
            model = model + factor * basis[b, m * tall : (m + 1) * tall]
        science = jnp.concatenate([exp_ref[:, at], edge_recv[1, 0:1, at], spare, edge_recv[0, 0:1, at]], axis=0)
        clean = jnp.concatenate(
            [mask_ref[:, at].astype(jnp.float32), edge_recv[1, 1:2, at], spare, edge_recv[0, 1:2, at]], axis=0
        )
        diff[:, at] = clean * (science - model)
    lane = lax.broadcasted_iota(jnp.int32, (rows, cols), 1)
    every = diff[...]
    mid = every[:rows]
    left = jnp.where(lane == 0, 0.0, turn(mid, 1, 1))
    right = jnp.where(lane == cols - 1, 0.0, turn(mid, -1, 1))
    around = turn(every, -1, 0)[:rows] + turn(every, 1, 0)[:rows] + right + left
    out_ref[...] = 4.0 * mid - around

    across.wait_send()
    for c in flying:
        c.wait_send()

    @pl.when(has_down)
    def _():
        halo(0).wait_send()
        edge(0).wait_send()
        relay(1).wait_send()

    @pl.when(has_up)
    def _():
        halo(1).wait_send()
        edge(1).wait_send()
        relay(0).wait_send()


def shards(template, exposure, cosmic_mask, stamp_blocks, row_filters, col_filters):
    rows, cols = exposure.shape[1:]
    bases, taps = row_filters.shape
    fit = 3 * bases + 7
    stripes = lax.axis_size("stripe")
    half = template.shape[1]
    ext_rows = 3 * rows
    wide = cols + 2 * EDGE
    tall = round_up(rows + 2, TILE)
    pad_b = round_up(bases, TILE)
    blocks = cols // (2 * EDGE)
    tiles = cols // EDGE
    radices = []
    rest = stripes
    while rest > 1:
        radices.append(min(rest, 8))
        rest //= radices[-1]
    slots = max(1, sum(r - 1 for r in radices))
    rounds = (stripes - 2).bit_length() if stripes > 2 else 0
    packed = fit // 4 + 1
    f32, bf16 = jnp.float32, jnp.bfloat16
    vmem = pl.BlockSpec(memory_space=pltpu.VMEM)
    anywhere = pl.BlockSpec(memory_space=pl.ANY)
    filtered, coef_row = pl.pallas_call(
        functools.partial(kernel, stripes, float(rows * stripes), radices, rounds),
        out_shape=(jax.ShapeDtypeStruct((rows, cols), f32), jax.ShapeDtypeStruct((1, fit), f32)),
        in_specs=[anywhere] * 6,
        out_specs=(vmem, vmem),
        scratch_shapes=[
            pltpu.VMEM((rows, half), f32),
            pltpu.VMEM((rows, cols), f32),
            pltpu.VMEM((rows, cols), jnp.int32),
            pltpu.SMEM(stamp_blocks.shape, jnp.int32),
            pltpu.VMEM((bases, taps), f32),
            pltpu.VMEM((bases, taps), f32),
            pltpu.VMEM((2, REACH, half), f32),
            pltpu.VMEM((2, REACH, half), f32),
            pltpu.VMEM((2, REACH, half), f32),
            pltpu.VMEM((rows, half), f32),
            pltpu.VMEM((2, 2, cols), f32),
            pltpu.VMEM((2, 2, cols), f32),
            pltpu.VMEM((ext_rows, wide), f32),
            pltpu.VMEM((bases * rows, 2 * EDGE), f32),
            pltpu.VMEM((bases * tall, 2 * EDGE), f32),
            pltpu.VMEM((bases, EDGE, 2 * EDGE), bf16),
            pltpu.VMEM((bases, 2 * EDGE, 4 * EDGE), bf16),
            pltpu.VMEM((bases * rows, cols), f32),
            pltpu.VMEM((blocks, rows * pad_b, EDGE), f32),
            pltpu.VMEM((blocks, rows * TILE, EDGE), f32),
            pltpu.VMEM((bases * tall, wide), f32),
            pltpu.VMEM((bases, tiles * tall, EDGE), f32),
            pltpu.VMEM((fit, EDGE), f32),
            pltpu.VMEM((bases, tall + TILE, EDGE), f32),
            pltpu.VMEM((tall, cols), f32),
            pltpu.VMEM((max(1, len(radices)), packed, EDGE), f32),
            pltpu.VMEM((slots, packed, EDGE), f32),
            pltpu.SemaphoreType.DMA((6,)),
            pltpu.SemaphoreType.DMA((7,)),
            pltpu.SemaphoreType.DMA((7,)),
            pltpu.SemaphoreType.DMA((slots,)),
            pltpu.SemaphoreType.DMA((slots,)),
            pltpu.SemaphoreType.REGULAR((max(1, rounds),)),
        ],
        compiler_params=pltpu.CompilerParams(collective_id=0, has_side_effects=True),
        name="fused",
    )(template, exposure[0], cosmic_mask[0], stamp_blocks, row_filters, col_filters)
    return (filtered[None], coef_row)


def solution(mesh):
    placed = (
        P(("groups", "stripe"), "exp"),
        P(("groups", "exp"), "stripe", None),
        P(("groups", "exp"), "stripe", None),
        P(("groups", "stripe"), None),
        P(),
        P(),
    )
    return jax.shard_map(
        shards,
        mesh=mesh,
        in_specs=placed,
        out_specs=(P(("groups", "exp"), "stripe", None), P(("groups", "exp"), None)),
        check_vma=False,
    )
```

time: 32.1 us -> 24 us (0.75)
  Pallas kernels: 31.3 us -> 21.1 us
  local copies, waits for them, and re-layouts: 0 us -> 2.08 us
    pallas_call x2 -> x1, Pallas kernels: 31.3 us -> 21.1 us  [shards(): pl.pallas_call(functools.partial(kernel, stripes, float(rows * stripes),...]
    unnamed x0 -> x4, local copies, waits for them, and re-layouts: none -> 2.08 us
where the time goes in v1:
time: 24 us; the launch traced here: 23.9 us
  Pallas kernels  21.1 us (88%)
  local copies, waits for them, and re-layouts  2.08 us (9%)
  between operations  0.65 us (3%)
    pallas_call x1, Pallas kernels, shards(): pl.pallas_call(functools.partial(kernel, stripes, float(rows * stripes),...  21.1 us
    unnamed x4, local copies, waits for them, and re-layouts  2.08 us

profile of v1, /device:TPU:0, one launch (start us, length us, event | category | flops | bytes accessed | tf_op | source)
XLA Modules:
  0.0 23.9 jit_solution(7374892140051683538)
XLA Ops:
  0.6 21.1 %fused.1 = (f32[16,2048]{1,0:T(8,128)}, f32[1,64]{1,0:T(1,128)}) custom-call(f32[16,1024]{1,0:T(8,128)} %tmpl_hbm.1, f32[16,2048]{1,0:T(8,128)} %bitcast.3, s32[16,2048]{1,0:T(8,128)} %bitcast.4, s32[1,16]{1,0:T(1,128)} %blk_hbm.1, f32[19,19]{1,0:T(8,128)} %rowf_hbm.1, f32[19,19]{1,0:T(8,128)} %colf_hbm.1), custom_call_target="tpu_custom_call" | custom-call | tf_op jit(solution)/shard_map/fused/pallas_call | solution.py:583
  21.8 0.0 copy-start
  21.8 1.6 %copy.10 = f32[1,16,2048]{2,1,0:T(8,128)} copy(f32[1,16,2048]{2,1,0:T(8,128)} %bitcast.5) | data formatting | bytes 262144
  23.4 0.0 copy-done
  23.4 0.5 %copy.11 = f32[1,64]{1,0:T(1,128)} copy(f32[1,64]{1,0:T(1,128)S(1)} %copy-done) | data formatting | bytes 512
Async XLA Ops:
  21.8 1.6 %copy-start = (f32[1,64]{1,0:T(1,128)S(1)}, f32[1,64]{1,0:T(1,128)}, u32[]{:S(2)}) copy-start(f32[1,64]{1,0:T(1,128)} %get-tuple-element.9) | copy-start | bytes 772

commit v2 on v1

--- a/solution.py
+++ b/solution.py
@@ -13,6 +13,7 @@
 TILE = 8
 BLOCK = 8
 REACH = HALF + 1
+VMEM_GRANT = 32 * 1024 * 1024
 MESH = pl.DeviceIdType.MESH
 LANE_DOT = (((1,), (1,)), ((), ()))
 
@@ -119,7 +120,7 @@
     blk_hbm,
     rowf_hbm,
     colf_hbm,
-    out_ref,
+    diff,
     row_ref,
     tmpl_ref,
     exp_ref,
@@ -145,7 +146,6 @@
     basis,
     coef_ref,
     plane,
-    diff,
     send,
     held,
     load_sem,
@@ -532,29 +532,34 @@
             [mask_ref[:, at].astype(jnp.float32), edge_recv[1, 1:2, at], spare, edge_recv[0, 1:2, at]], axis=0
         )
         diff[:, at] = clean * (science - model)
+
+    across.wait_send()
+    for c in flying:
+        c.wait_send()
+
+    @pl.when(has_down)
+    def _():
+        halo(0).wait_send()
+        edge(0).wait_send()
+        relay(1).wait_send()
+
+    @pl.when(has_up)
+    def _():
+        halo(1).wait_send()
+        edge(1).wait_send()
+        relay(0).wait_send()
+
+
+def finish_kernel(diff_ref, coef_ref, out_ref, row_ref):
+    rows, cols = out_ref.shape
     lane = lax.broadcasted_iota(jnp.int32, (rows, cols), 1)
-    every = diff[...]
+    every = diff_ref[...]
     mid = every[:rows]
     left = jnp.where(lane == 0, 0.0, turn(mid, 1, 1))
     right = jnp.where(lane == cols - 1, 0.0, turn(mid, -1, 1))
     around = turn(every, -1, 0)[:rows] + turn(every, 1, 0)[:rows] + right + left
     out_ref[...] = 4.0 * mid - around
-
-    across.wait_send()
-    for c in flying:
-        c.wait_send()
-
-    @pl.when(has_down)
-    def _():
-        halo(0).wait_send()
-        edge(0).wait_send()
-        relay(1).wait_send()
-
-    @pl.when(has_up)
-    def _():
-        halo(1).wait_send()
-        edge(1).wait_send()
-        relay(0).wait_send()
+    row_ref[...] = coef_ref[...]
 
 
 def shards(template, exposure, cosmic_mask, stamp_blocks, row_filters, col_filters):
@@ -579,10 +584,12 @@
     packed = fit // 4 + 1
     f32, bf16 = jnp.float32, jnp.bfloat16
     vmem = pl.BlockSpec(memory_space=pltpu.VMEM)
-    anywhere = pl.BlockSpec(memory_space=pl.ANY)
-    filtered, coef_row = pl.pallas_call(
+    anywhere = pl.BlockSpec(memory_space=pltpu.HBM)
+    operands = (template, exposure[0], cosmic_mask[0], stamp_blocks, row_filters, col_filters)
+    operands = [pltpu.with_memory_space_constraint(x, pltpu.HBM) for x in operands]
+    diff, coef_row = pl.pallas_call(
         functools.partial(kernel, stripes, float(rows * stripes), radices, rounds),
-        out_shape=(jax.ShapeDtypeStruct((rows, cols), f32), jax.ShapeDtypeStruct((1, fit), f32)),
+        out_shape=(jax.ShapeDtypeStruct((tall, cols), f32), jax.ShapeDtypeStruct((1, fit), f32)),
         in_specs=[anywhere] * 6,
         out_specs=(vmem, vmem),
         scratch_shapes=[
@@ -610,7 +617,6 @@
             pltpu.VMEM((bases, tiles * tall, EDGE), f32),
             pltpu.VMEM((fit, EDGE), f32),
             pltpu.VMEM((bases, tall + TILE, EDGE), f32),
-            pltpu.VMEM((tall, cols), f32),
             pltpu.VMEM((max(1, len(radices)), packed, EDGE), f32),
             pltpu.VMEM((slots, packed, EDGE), f32),
             pltpu.SemaphoreType.DMA((6,)),
@@ -620,9 +626,19 @@
             pltpu.SemaphoreType.DMA((slots,)),
             pltpu.SemaphoreType.REGULAR((max(1, rounds),)),
         ],
-        compiler_params=pltpu.CompilerParams(collective_id=0, has_side_effects=True),
+        compiler_params=pltpu.CompilerParams(
+            collective_id=0, has_side_effects=True, vmem_limit_bytes=VMEM_GRANT
+        ),
         name="fused",
-    )(template, exposure[0], cosmic_mask[0], stamp_blocks, row_filters, col_filters)
+    )(*operands)
+    filtered, coef_row = pl.pallas_call(
+        finish_kernel,
+        out_shape=(jax.ShapeDtypeStruct((rows, cols), f32), jax.ShapeDtypeStruct((1, fit), f32)),
+        in_specs=[vmem, vmem],
+        out_specs=(vmem, vmem),
+        compiler_params=pltpu.CompilerParams(vmem_limit_bytes=VMEM_GRANT),
+        name="finish",
+    )(diff, coef_row)
     return (filtered[None], coef_row)
 
 

time: 24 us -> 22 us (0.917)
  local copies, waits for them, and re-layouts: 2.08 us -> 0 us
    unnamed x4 -> x0, local copies, waits for them, and re-layouts: 2.08 us -> none
    pallas_call x0 -> x1, Pallas kernels: none -> 0.8 us  [shards(): pl.pallas_call(finish_kernel, out_shape=(jax.ShapeDtypeStruct((rows, cols...]
    pallas_call x1, Pallas kernels: 21.1 us -> 20.4 us  [shards(): pl.pallas_call(functools.partial(kernel, stripes, float(rows * stripes),...]
where the time goes in v2:
time: 22 us; the launch traced here: 21.8 us
  Pallas kernels  21.2 us (96%)
  between operations  0.64 us (3%)
    pallas_call x1, Pallas kernels, shards(): pl.pallas_call(functools.partial(kernel, stripes, float(rows * stripes),...  20.4 us
    pallas_call x1, Pallas kernels, shards(): pl.pallas_call(finish_kernel, out_shape=(jax.ShapeDtypeStruct((rows, cols...  0.8 us

profile of v2, /device:TPU:0, one launch (start us, length us, event | category | flops | bytes accessed | tf_op | source)
XLA Modules:
  0.0 21.8 jit_solution(15696137195682747827)
XLA Ops:
  0.6 20.4 %fused.1 = (f32[24,2048]{1,0:T(8,128)S(1)}, f32[1,64]{1,0:T(1,128)S(1)}) custom-call(f32[16,1024]{1,0:T(8,128)} %tmpl_hbm.1, f32[16,2048]{1,0:T(8,128)} %bitcast.3, s32[16,2048]{1,0:T(8,128)} %bitcast.4, s32[1,16]{1,0:T(1,128)} %blk_hbm.1, f32[19,19]{1,0:T(8,128)} %rowf_hbm.1, f32[19,19]{1,0:T(8,128)} %colf_hbm.1), custom_call_target="tpu_custom_call" | custom-call | tf_op jit(solution)/shard_map/fused/pallas_call | solution.py:590
  21.1 0.8 %finish.1 = (f32[16,2048]{1,0:T(8,128)}, f32[1,64]{1,0:T(1,128)}) custom-call(f32[24,2048]{1,0:T(8,128)S(1)} %get-tuple-element.6.diff_ref, f32[1,64]{1,0:T(1,128)S(1)} %get-tuple-element.7.coef_ref), custom_call_target="tpu_custom_call" | custom-call | tf_op jit(solution)/shard_map/finish/pallas_call | solution.py:634

commit v3 on v2

--- a/solution.py
+++ b/solution.py
@@ -142,6 +142,9 @@
     vert,
     design,
     ground,
+    clear,
+    across_u,
+    grams,
     vert_f,
     basis,
     coef_ref,
@@ -261,14 +264,6 @@
     across = copy(tmpl_ref, whole, 6, me, 1 - core)
     across.start()
 
-    @pl.when(has_down)
-    def _():
-        edge(0).start()
-
-    @pl.when(has_up)
-    def _():
-        edge(1).start()
-
     def call(n):
         reach = 1 << n
 
@@ -330,6 +325,11 @@
         lower = jnp.concatenate([f_rest, jnp.zeros_like(f_rest)], axis=1)
         toep_f[b] = jnp.concatenate([upper, lower], axis=0)
 
+    if rounds:
+        listen(0)
+    if rounds > 1:
+        call(1)
+
     first = (me * rows).astype(jnp.float32)
     index = lax.broadcasted_iota(jnp.int32, (rows, 1), 0).astype(jnp.float32)
     v = jnp.broadcast_to(row_coords(index + first, region_rows), (rows, half_cols))
@@ -337,6 +337,9 @@
     u_sel = pick(u_all)
     u = jnp.concatenate([u_sel] * (rows // TILE), axis=0)
     good = pick(mask_ref[...].astype(jnp.float32))
+    for m in range(blocks):
+        clear[m] = good[:, m * EDGE : (m + 1) * EDGE]
+        across_u[m] = u_sel[:, m * EDGE : (m + 1) * EDGE]
     terms = background(u, v)
     terms[0] = jnp.ones_like(u)
     terms.append(pick(exp_ref[...]))
@@ -349,11 +352,6 @@
         for m in range(blocks):
             design[m, pl.ds(b, rows, stride=pad_b), :] = zero
 
-    if rounds:
-        listen(0)
-    if rounds > 1:
-        call(1)
-
     @pl.when(has_up)
     def _():
         halo(0).wait_recv()
@@ -364,38 +362,14 @@
         halo(1).wait_recv()
         relay(1).start()
 
-    across.wait_recv()
     mine = pl.ds(pl.multiple_of(EDGE + core * half, EDGE), half)
     theirs = pl.ds(pl.multiple_of(EDGE + (1 - core) * half, EDGE), half)
-    ext_ref[rows : 2 * rows, mine] = tmpl_ref[...]
-    ext_ref[rows : 2 * rows, theirs] = whole[...]
-
-    @pl.when(has_up)
-    def _():
-        relay(0).wait_recv()
-
-    @pl.when(has_down)
-    def _():
-        relay(1).wait_recv()
-
-    for n, (buf, where) in enumerate(((halo_own, mine), (halo_other, theirs))):
+
+    def settle(where, body, buf):
+        ext_ref[rows : 2 * rows, where] = body[...]
         ext_ref[rows - TILE : rows, where] = buf[0, 0:TILE]
         ext_ref[rows - REACH : rows - TILE, where] = buf[0, TILE:REACH]
         ext_ref[2 * rows : 2 * rows + REACH, where] = buf[1]
-    ext = turn(ext_ref[...], -(EDGE - HALF), 1)
-    ext_ref[...] = ext
-
-    for n in range(1, rounds):
-        listen(n)
-        if n + 1 < rounds:
-            call(n + 1)
-
-    windows = []
-    for s in range(stamps):
-        early = ext[:, s * EDGE : (s + 1) * EDGE]
-        after = ext[:, (s + 1) * EDGE : (s + 2) * EDGE]
-        late = pltpu.roll(jnp.where(low, after, early), STAMP_W, 1)
-        windows.append(jnp.where(parity[s], late, early))
 
     def stack(x):
         high, rest = split(x)
@@ -403,34 +377,84 @@
         gap2 = jnp.zeros((EDGE - ext_rows, x.shape[1]), jnp.bfloat16)
         return jnp.concatenate([high, rest, gap, high, gap2], axis=0)
 
-    window = jnp.concatenate(windows, axis=1)
-    vert[...] = jnp.dot(bandw[...].astype(jnp.bfloat16), stack(window), preferred_element_type=jnp.float32)
-
-    for b in range(bases):
-        x = vert[b * rows : (b + 1) * rows, :]
-        x = jnp.concatenate([x[:, s * EDGE : (s + 1) * EDGE] for s in range(stamps)], axis=0)
-        y = lax.dot_general(
-            jnp.concatenate(split(x), axis=1), toep_s[b], LANE_DOT, preferred_element_type=jnp.float32
-        )
-        y = y + pltpu.roll(y, STAMP_W, 1)
-        for m in range(blocks):
-            picked = jnp.where(low, y[2 * m * rows : (2 * m + 1) * rows], y[(2 * m + 1) * rows : (2 * m + 2) * rows])
-            design[m, pl.ds(b, rows, stride=pad_b), :] = picked * good[:, m * EDGE : (m + 1) * EDGE]
-
     total = 3 * pad_b + TILE
-    acc = jnp.zeros((total, total), jnp.float32)
-    for r in range(rows):
-        parts = []
-        for m in range(blocks):
-            d = design[m, r * pad_b : (r + 1) * pad_b, :]
-            um = u_sel[0:1, m * EDGE : (m + 1) * EDGE]
-            vm = v[r : r + 1, 0:EDGE]
-            parts.append(jnp.concatenate([d, d * um, d * vm, ground[m, r * TILE : (r + 1) * TILE, :]], axis=0))
-        x = jnp.concatenate(parts, axis=1).astype(jnp.bfloat16)
-        acc = acc + lax.dot_general(x, x, LANE_DOT, preferred_element_type=jnp.float32)
+
+    def stamp_sums(first_block, n, slot):
+        span = 2 * n * EDGE
+        at = pl.multiple_of(first_block * 2 * EDGE, EDGE)
+        ext = turn(ext_ref[:, pl.ds(at, span + 2 * EDGE)], -(EDGE - HALF), 1)
+        windows = []
+        for s in range(2 * n):
+            odd = blk_ref[0, 2 * first_block + s] % 2 == 1
+            early = ext[:, s * EDGE : (s + 1) * EDGE]
+            after = ext[:, (s + 1) * EDGE : (s + 2) * EDGE]
+            late = pltpu.roll(jnp.where(low, after, early), STAMP_W, 1)
+            windows.append(jnp.where(odd, late, early))
+        window = jnp.concatenate(windows, axis=1)
+        vert[:, :span] = jnp.dot(bandw[...].astype(jnp.bfloat16), stack(window), preferred_element_type=jnp.float32)
+        for b in range(bases):
+            x = vert[b * rows : (b + 1) * rows, :span]
+            x = jnp.concatenate([x[:, s * EDGE : (s + 1) * EDGE] for s in range(2 * n)], axis=0)
+            y = lax.dot_general(
+                jnp.concatenate(split(x), axis=1), toep_s[b], LANE_DOT, preferred_element_type=jnp.float32
+            )
+            y = y + pltpu.roll(y, STAMP_W, 1)
+            for m in range(n):
+                near, far = y[2 * m * rows : (2 * m + 1) * rows], y[(2 * m + 1) * rows : (2 * m + 2) * rows]
+                design[m, pl.ds(b, rows, stride=pad_b), :] = jnp.where(low, near, far) * clear[first_block + m]
+        sums = [jnp.zeros((total, total), jnp.float32) for _ in range(2)]
+        for pair in range(rows // 2):
+            parts = []
+            for r in (2 * pair, 2 * pair + 1):
+                vm = v[r : r + 1, 0:EDGE]
+                for m in range(n):
+                    d = design[m, r * pad_b : (r + 1) * pad_b, :]
+                    um = across_u[first_block + m, 0:1]
+                    rest = ground[first_block + m, r * TILE : (r + 1) * TILE, :]
+                    parts.append(jnp.concatenate([d, d * um, d * vm, rest], axis=0))
+            x = jnp.concatenate(parts, axis=1).astype(jnp.bfloat16)
+            sums[pair % 2] = sums[pair % 2] + lax.dot_general(x, x, LANE_DOT, preferred_element_type=jnp.float32)
+        for h in range(2):
+            grams[slot + h, :, 0:total] = sums[h]
+
+    settle(mine, tmpl_ref, halo_own)
+    ahead = blocks // 2 - 1
+    if ahead:
+        stamp_sums(core * (blocks - ahead), ahead, 0)
+    if rounds > 1:
+        listen(1)
+    if rounds > 2:
+        call(2)
+    across.wait_recv()
+
+    @pl.when(has_up)
+    def _():
+        relay(0).wait_recv()
+
+    @pl.when(has_down)
+    def _():
+        relay(1).wait_recv()
+
+    settle(theirs, whole, halo_other)
+    stamp_sums((1 - core) * ahead, blocks - ahead, 2)
+    @pl.when(has_down)
+    def _():
+        edge(0).start()
+
+    @pl.when(has_up)
+    def _():
+        edge(1).start()
+
+    acc = grams[2, :, 0:total] + grams[3, :, 0:total]
+    if ahead:
+        acc = acc + (grams[0, :, 0:total] + grams[1, :, 0:total])
     gram = jnp.concatenate([acc, jnp.zeros((total, EDGE - total), jnp.float32)], axis=1)
     gram = squeeze_terms(squeeze_terms(gram, bases, 0), bases, 1)
     body, last = pack_normal(gram, fit)
+    for n in range(2, rounds):
+        listen(n)
+        if n + 1 < rounds:
+            call(n + 1)
 
     def reduce_start(phase, base, stride, radix):
         digit = (me // stride) % radix
@@ -472,7 +496,7 @@
         flying += copies
         if phase == 0:
             vert_f[...] = jnp.dot(
-                bandf[...].astype(jnp.bfloat16), stack(ext_ref[...]), preferred_element_type=jnp.float32
+                bandf[...].astype(jnp.bfloat16), stack(turn(ext_ref[...], -(EDGE - HALF), 1)), preferred_element_type=jnp.float32
             )
             for b in range(bases):
                 x = vert_f[b * tall : (b + 1) * tall, :]
@@ -613,6 +637,9 @@
             pltpu.VMEM((bases * rows, cols), f32),
             pltpu.VMEM((blocks, rows * pad_b, EDGE), f32),
             pltpu.VMEM((blocks, rows * TILE, EDGE), f32),
+            pltpu.VMEM((blocks, rows, EDGE), f32),
+            pltpu.VMEM((blocks, TILE, EDGE), f32),
+            pltpu.VMEM((4, 3 * pad_b + TILE, EDGE), f32),
             pltpu.VMEM((bases * tall, wide), f32),
             pltpu.VMEM((bases, tiles * tall, EDGE), f32),
             pltpu.VMEM((fit, EDGE), f32),

time: 22 us -> 20.4 us (0.927)
  Pallas kernels: 21.2 us -> 19.6 us
    pallas_call x1, Pallas kernels: 20.4 us -> 18.8 us  [shards(): pl.pallas_call(functools.partial(kernel, stripes, float(rows * stripes),...]
where the time goes in v3:
time: 20.4 us; the launch traced here: 20.2 us
  Pallas kernels  19.6 us (96%)
  between operations  0.64 us (3%)
    pallas_call x1, Pallas kernels, shards(): pl.pallas_call(functools.partial(kernel, stripes, float(rows * stripes),...  18.8 us
    pallas_call x1, Pallas kernels, shards(): pl.pallas_call(finish_kernel, out_shape=(jax.ShapeDtypeStruct((rows, cols...  0.8 us

profile of v3, /device:TPU:0, one launch (start us, length us, event | category | flops | bytes accessed | tf_op | source)
XLA Modules:
  0.0 20.2 jit_solution(9500147882381294366)
XLA Ops:
  0.6 18.8 %fused.1 = (f32[24,2048]{1,0:T(8,128)S(1)}, f32[1,64]{1,0:T(1,128)S(1)}) custom-call(f32[16,1024]{1,0:T(8,128)} %tmpl_hbm.1, f32[16,2048]{1,0:T(8,128)} %bitcast.3, s32[16,2048]{1,0:T(8,128)} %bitcast.4, s32[1,16]{1,0:T(1,128)} %blk_hbm.1, f32[19,19]{1,0:T(8,128)} %rowf_hbm.1, f32[19,19]{1,0:T(8,128)} %colf_hbm.1), custom_call_target="tpu_custom_call" | custom-call | tf_op jit(solution)/shard_map/fused/pallas_call | solution.py:614
  19.4 0.8 %finish.1 = (f32[16,2048]{1,0:T(8,128)}, f32[1,64]{1,0:T(1,128)}) custom-call(f32[24,2048]{1,0:T(8,128)S(1)} %get-tuple-element.6.diff_ref, f32[1,64]{1,0:T(1,128)S(1)} %get-tuple-element.7.coef_ref), custom_call_target="tpu_custom_call" | custom-call | tf_op jit(solution)/shard_map/finish/pallas_call | solution.py:661

commit v4 on v3

--- a/solution.py
+++ b/solution.py
@@ -95,18 +95,30 @@
 
 
 def eliminate(a, fit):
-    sub = lax.broadcasted_iota(jnp.int32, a.shape, 0)
-    for first in range(0, fit, BLOCK):
-        block = range(first, min(first + BLOCK, fit))
-        cols = [jnp.broadcast_to(a[:, k : k + 1], a.shape) for k in block]
-        for t, k in enumerate(block):
-            inverse = pl.reciprocal(cols[t][k : k + 1, :])
-            row = a[k : k + 1, :] * inverse
-            a = jnp.where(sub == k, row, a - cols[t] * row)
-            for w in range(t + 1, len(block)):
-                factor = cols[w][k : k + 1, :] * inverse
-                cols[w] = jnp.where(sub == k, factor, cols[w] - cols[t] * factor)
-    return jnp.broadcast_to(a[:, fit : fit + 1], a.shape)
+    shape = (TILE, EDGE)
+    count = fit // TILE
+    tiles = [a[i * TILE : (i + 1) * TILE] for i in range(count)]
+    sub = lax.broadcasted_iota(jnp.int32, shape, 0)
+    for i in range(count):
+        order = [j % count for j in range(i, i + count)]
+        cols = {j: [jnp.broadcast_to(tiles[j][:, k : k + 1], shape) for k in range(i * TILE, (i + 1) * TILE)] for j in order}
+        near = list(cols[i])
+        for t in range(TILE):
+            inverse = pl.reciprocal(near[t][t : t + 1])
+
+            def step(x):
+                row = x[t : t + 1] * inverse
+                return jnp.where(sub == t, row, x - near[t] * row)
+
+            for w in range(t + 1, TILE):
+                near[w] = step(near[w])
+            tiles[i] = step(tiles[i])
+        for j in order[1:]:
+            terms = [cols[j][t] * tiles[i][t : t + 1] for t in range(TILE)]
+            while len(terms) > 1:
+                terms = [terms[q] + terms[q + 1] for q in range(0, len(terms), 2)]
+            tiles[j] = tiles[j] - terms[0]
+    return jnp.concatenate([jnp.broadcast_to(x[:, fit : fit + 1], shape) for x in tiles], axis=0)
 
 
 def kernel(
@@ -241,11 +253,17 @@
         return copy(halo_own.at[way], halo_other.at[way], 4 + way, me, 1 - core)
 
     more = REACH - TILE
+    spans = half // EDGE
     for c in loads:
         c.wait()
-    halo_send[0, 0:TILE] = tmpl_ref[rows - TILE : rows]
-    halo_send[0, TILE:REACH] = tmpl_ref[rows - REACH : rows - TILE]
-    halo_send[1] = tmpl_ref[0:REACH]
+    for way, near, far in ((0, rows - TILE, rows - REACH), (1, 0, TILE)):
+        halo_send[way, :, 0:half] = tmpl_ref[near : near + TILE]
+        for e in range(more):
+            for m in range(spans):
+                column, line = half + (e * spans + m) // TILE * EDGE, (e * spans + m) % TILE
+                halo_send[way, line : line + 1, column : column + EDGE] = tmpl_ref[
+                    far + e : far + e + 1, m * EDGE : (m + 1) * EDGE
+                ]
     edge_send[0, 0:1, :] = exp_ref[rows - 1 : rows, :]
     edge_send[0, 1:2, :] = mask_ref[rows - 1 : rows, :].astype(jnp.float32)
     edge_send[1, 0:1, :] = exp_ref[0:1, :]
@@ -362,14 +380,16 @@
         halo(1).wait_recv()
         relay(1).start()
 
-    mine = pl.ds(pl.multiple_of(EDGE + core * half, EDGE), half)
-    theirs = pl.ds(pl.multiple_of(EDGE + (1 - core) * half, EDGE), half)
-
-    def settle(where, body, buf):
+    def settle(side, body, buf):
+        where = pl.ds(pl.multiple_of(EDGE + side * half, EDGE), half)
         ext_ref[rows : 2 * rows, where] = body[...]
-        ext_ref[rows - TILE : rows, where] = buf[0, 0:TILE]
-        ext_ref[rows - REACH : rows - TILE, where] = buf[0, TILE:REACH]
-        ext_ref[2 * rows : 2 * rows + REACH, where] = buf[1]
+        for way, near, far in ((0, rows - TILE, rows - REACH), (1, 2 * rows, 2 * rows + TILE)):
+            ext_ref[near : near + TILE, where] = buf[way, :, 0:half]
+            for e in range(more):
+                for m in range(spans):
+                    column, line = half + (e * spans + m) // TILE * EDGE, (e * spans + m) % TILE
+                    at = pl.ds(pl.multiple_of((1 + m) * EDGE + side * half, EDGE), EDGE)
+                    ext_ref[far + e : far + e + 1, at] = buf[way, line : line + 1, column : column + EDGE]
 
     def stack(x):
         high, rest = split(x)
@@ -417,7 +437,7 @@
         for h in range(2):
             grams[slot + h, :, 0:total] = sums[h]
 
-    settle(mine, tmpl_ref, halo_own)
+    settle(core, tmpl_ref, halo_own)
     ahead = blocks // 2 - 1
     if ahead:
         stamp_sums(core * (blocks - ahead), ahead, 0)
@@ -435,7 +455,7 @@
     def _():
         relay(1).wait_recv()
 
-    settle(theirs, whole, halo_other)
+    settle(1 - core, whole, halo_other)
     stamp_sums((1 - core) * ahead, blocks - ahead, 2)
     @pl.when(has_down)
     def _():
@@ -606,6 +626,7 @@
     slots = max(1, sum(r - 1 for r in radices))
     rounds = (stripes - 2).bit_length() if stripes > 2 else 0
     packed = fit // 4 + 1
+    extra = round_up((REACH - TILE) * half // EDGE, TILE) // TILE * EDGE
     f32, bf16 = jnp.float32, jnp.bfloat16
     vmem = pl.BlockSpec(memory_space=pltpu.VMEM)
     anywhere = pl.BlockSpec(memory_space=pltpu.HBM)
@@ -623,9 +644,9 @@
             pltpu.SMEM(stamp_blocks.shape, jnp.int32),
             pltpu.VMEM((bases, taps), f32),
             pltpu.VMEM((bases, taps), f32),
-            pltpu.VMEM((2, REACH, half), f32),
-            pltpu.VMEM((2, REACH, half), f32),
-            pltpu.VMEM((2, REACH, half), f32),
+            pltpu.VMEM((2, TILE, half + extra), f32),
+            pltpu.VMEM((2, TILE, half + extra), f32),
+            pltpu.VMEM((2, TILE, half + extra), f32),
             pltpu.VMEM((rows, half), f32),
             pltpu.VMEM((2, 2, cols), f32),
             pltpu.VMEM((2, 2, cols), f32),

time: 20.4 us -> 19.7 us (0.966)
  Pallas kernels: 19.6 us -> 18.9 us
    pallas_call x1, Pallas kernels: 18.8 us -> 18.1 us  [shards(): pl.pallas_call(functools.partial(kernel, stripes, float(rows * stripes),...]
where the time goes in v4:
time: 19.7 us; the launch traced here: 19.5 us
  Pallas kernels  18.9 us (96%)
  between operations  0.64 us (3%)
    pallas_call x1, Pallas kernels, shards(): pl.pallas_call(functools.partial(kernel, stripes, float(rows * stripes),...  18.1 us
    pallas_call x1, Pallas kernels, shards(): pl.pallas_call(finish_kernel, out_shape=(jax.ShapeDtypeStruct((rows, cols...  0.8 us

profile of v4, /device:TPU:0, one launch (start us, length us, event | category | flops | bytes accessed | tf_op | source)
XLA Modules:
  0.0 19.5 jit_solution(7805003645326349376)
XLA Ops:
  0.6 18.1 %fused.1 = (f32[24,2048]{1,0:T(8,128)S(1)}, f32[1,64]{1,0:T(1,128)S(1)}) custom-call(f32[16,1024]{1,0:T(8,128)} %tmpl_hbm.1, f32[16,2048]{1,0:T(8,128)} %bitcast.3, s32[16,2048]{1,0:T(8,128)} %bitcast.4, s32[1,16]{1,0:T(1,128)} %blk_hbm.1, f32[19,19]{1,0:T(8,128)} %rowf_hbm.1, f32[19,19]{1,0:T(8,128)} %colf_hbm.1), custom_call_target="tpu_custom_call" | custom-call | tf_op jit(solution)/shard_map/fused/pallas_call | solution.py:635
  18.7 0.8 %finish.1 = (f32[16,2048]{1,0:T(8,128)}, f32[1,64]{1,0:T(1,128)}) custom-call(f32[24,2048]{1,0:T(8,128)S(1)} %get-tuple-element.6.diff_ref, f32[1,64]{1,0:T(1,128)S(1)} %get-tuple-element.7.coef_ref), custom_call_target="tpu_custom_call" | custom-call | tf_op jit(solution)/shard_map/finish/pallas_call | solution.py:682

commit v5 on v4

--- a/solution.py
+++ b/solution.py
@@ -14,6 +14,7 @@
 BLOCK = 8
 REACH = HALF + 1
 VMEM_GRANT = 32 * 1024 * 1024
+GRAM_EARLY = 2
 MESH = pl.DeviceIdType.MESH
 LANE_DOT = (((1,), (1,)), ((), ()))
 
@@ -399,7 +400,7 @@
 
     total = 3 * pad_b + TILE
 
-    def stamp_sums(first_block, n, slot):
+    def stamp_design(first_block, n, place):
         span = 2 * n * EDGE
         at = pl.multiple_of(first_block * 2 * EDGE, EDGE)
         ext = turn(ext_ref[:, pl.ds(at, span + 2 * EDGE)], -(EDGE - HALF), 1)
@@ -418,17 +419,19 @@
             y = lax.dot_general(
                 jnp.concatenate(split(x), axis=1), toep_s[b], LANE_DOT, preferred_element_type=jnp.float32
             )
-            y = y + pltpu.roll(y, STAMP_W, 1)
             for m in range(n):
                 near, far = y[2 * m * rows : (2 * m + 1) * rows], y[(2 * m + 1) * rows : (2 * m + 2) * rows]
-                design[m, pl.ds(b, rows, stride=pad_b), :] = jnp.where(low, near, far) * clear[first_block + m]
+                picked = jnp.where(low, near, far) + pltpu.roll(jnp.where(low, far, near), STAMP_W, 1)
+                design[place + m, pl.ds(b, rows, stride=pad_b), :] = picked * clear[first_block + m]
+
+    def stamp_gram(first_block, n, place, pairs, slot):
         sums = [jnp.zeros((total, total), jnp.float32) for _ in range(2)]
-        for pair in range(rows // 2):
+        for pair in pairs:
             parts = []
             for r in (2 * pair, 2 * pair + 1):
                 vm = v[r : r + 1, 0:EDGE]
                 for m in range(n):
-                    d = design[m, r * pad_b : (r + 1) * pad_b, :]
+                    d = design[place + m, r * pad_b : (r + 1) * pad_b, :]
                     um = across_u[first_block + m, 0:1]
                     rest = ground[first_block + m, r * TILE : (r + 1) * TILE, :]
                     parts.append(jnp.concatenate([d, d * um, d * vm, rest], axis=0))
@@ -439,8 +442,11 @@
 
     settle(core, tmpl_ref, halo_own)
     ahead = blocks // 2 - 1
+    pairs = range(rows // 2)
+    near_block, far_block = core * (blocks - ahead), (1 - core) * ahead
     if ahead:
-        stamp_sums(core * (blocks - ahead), ahead, 0)
+        stamp_design(near_block, ahead, 0)
+        stamp_gram(near_block, ahead, 0, pairs[:GRAM_EARLY], 0)
     if rounds > 1:
         listen(1)
     if rounds > 2:
@@ -456,7 +462,10 @@
         relay(1).wait_recv()
 
     settle(1 - core, whole, halo_other)
-    stamp_sums((1 - core) * ahead, blocks - ahead, 2)
+    if ahead:
+        stamp_gram(near_block, ahead, 0, pairs[GRAM_EARLY:], 2)
+    stamp_design(far_block, blocks - ahead, ahead)
+    stamp_gram(far_block, blocks - ahead, ahead, pairs, 4)
     @pl.when(has_down)
     def _():
         edge(0).start()
@@ -465,9 +474,9 @@
     def _():
         edge(1).start()
 
-    acc = grams[2, :, 0:total] + grams[3, :, 0:total]
+    acc = grams[4, :, 0:total] + grams[5, :, 0:total]
     if ahead:
-        acc = acc + (grams[0, :, 0:total] + grams[1, :, 0:total])
+        acc = acc + ((grams[0, :, 0:total] + grams[1, :, 0:total]) + (grams[2, :, 0:total] + grams[3, :, 0:total]))
     gram = jnp.concatenate([acc, jnp.zeros((total, EDGE - total), jnp.float32)], axis=1)
     gram = squeeze_terms(squeeze_terms(gram, bases, 0), bases, 1)
     body, last = pack_normal(gram, fit)
@@ -660,7 +669,7 @@
             pltpu.VMEM((blocks, rows * TILE, EDGE), f32),
             pltpu.VMEM((blocks, rows, EDGE), f32),
             pltpu.VMEM((blocks, TILE, EDGE), f32),
-            pltpu.VMEM((4, 3 * pad_b + TILE, EDGE), f32),
+            pltpu.VMEM((6, 3 * pad_b + TILE, EDGE), f32),
             pltpu.VMEM((bases * tall, wide), f32),
             pltpu.VMEM((bases, tiles * tall, EDGE), f32),
             pltpu.VMEM((fit, EDGE), f32),

time: 19.7 us -> 19.5 us (0.990)
  Pallas kernels: 18.9 us -> 18.7 us
where the time goes in v5:
time: 19.5 us; the launch traced here: 19.4 us
  Pallas kernels  18.7 us (96%)
  between operations  0.64 us (3%)
    pallas_call x1, Pallas kernels, shards(): pl.pallas_call(functools.partial(kernel, stripes, float(rows * stripes),...  17.9 us
    pallas_call x1, Pallas kernels, shards(): pl.pallas_call(finish_kernel, out_shape=(jax.ShapeDtypeStruct((rows, cols...  0.8 us

profile of v5, /device:TPU:0, one launch (start us, length us, event | category | flops | bytes accessed | tf_op | source)
XLA Modules:
  0.0 19.4 jit_solution(9961095027990546129)
XLA Ops:
  0.6 17.9 %fused.1 = (f32[24,2048]{1,0:T(8,128)S(1)}, f32[1,64]{1,0:T(1,128)S(1)}) custom-call(f32[16,1024]{1,0:T(8,128)} %tmpl_hbm.1, f32[16,2048]{1,0:T(8,128)} %bitcast.3, s32[16,2048]{1,0:T(8,128)} %bitcast.4, s32[1,16]{1,0:T(1,128)} %blk_hbm.1, f32[19,19]{1,0:T(8,128)} %rowf_hbm.1, f32[19,19]{1,0:T(8,128)} %colf_hbm.1), custom_call_target="tpu_custom_call" | custom-call | tf_op jit(solution)/shard_map/fused/pallas_call | solution.py:644
  18.6 0.8 %finish.1 = (f32[16,2048]{1,0:T(8,128)}, f32[1,64]{1,0:T(1,128)}) custom-call(f32[24,2048]{1,0:T(8,128)S(1)} %get-tuple-element.6.diff_ref, f32[1,64]{1,0:T(1,128)S(1)} %get-tuple-element.7.coef_ref), custom_call_target="tpu_custom_call" | custom-call | tf_op jit(solution)/shard_map/finish/pallas_call | solution.py:691

commit v6 on v5

--- a/solution.py
+++ b/solution.py
@@ -162,6 +162,7 @@
     basis,
     coef_ref,
     plane,
+    clean_ref,
     send,
     held,
     load_sem,
@@ -518,7 +519,26 @@
             values = [values[q] + values[q + 1] for q in range(0, len(values), 2)]
         return values[0]
 
+    def prepare():
+        for c in (0, 1):
+
+            @pl.when((has_up, has_down)[c])
+            def _():
+                edge(c).wait_recv()
+
+        spare = jnp.zeros((tall - rows - 2, EDGE), jnp.float32)
+        for m in range(tiles):
+            at = slice(m * EDGE, (m + 1) * EDGE)
+            science = jnp.concatenate([exp_ref[:, at], edge_recv[1, 0:1, at], spare, edge_recv[0, 0:1, at]], axis=0)
+            clean = jnp.concatenate(
+                [mask_ref[:, at].astype(jnp.float32), edge_recv[1, 1:2, at], spare, edge_recv[0, 1:2, at]], axis=0
+            )
+            clean_ref[:, at] = clean
+            diff[:, at] = clean * science
+
     base, stride, flying = 0, 1, []
+    if not radices:
+        prepare()
     for phase, radix in enumerate(radices):
         put(phase, (body, last))
         copies = reduce_start(phase, base, stride, radix)
@@ -534,6 +554,7 @@
                     jnp.concatenate(split(x), axis=1), toep_f[b], LANE_DOT, preferred_element_type=jnp.float32
                 )
                 basis[b] = y[:, :EDGE] + y[:, EDGE:]
+            prepare()
         for c in copies:
             c.wait_recv()
         body = tree([send[phase, 0:fold]] + [held[base + k, 0:fold] for k in range(radix - 1)])
@@ -548,11 +569,6 @@
     spot = jnp.where(n < 3 * bases, 3 * (n - bases * term) + term, n)
     same = spot == lax.broadcasted_iota(jnp.int32, (fit, fit), 1)
     row_ref[...] = jnp.sum(jnp.where(same, answer[:, :fit], 0.0), axis=0, keepdims=True)
-
-    for c in (0, 1):
-        @pl.when((has_up, has_down)[c])
-        def _():
-            edge(c).wait_recv()
 
     def coef(n):
         return coef_ref[pl.ds(n, TILE, stride=0), :]
@@ -571,7 +587,6 @@
     flat = three(q[0]) + v * three(q[2]) + vv * three(q[5])
     slope = three(q[1]) + v * three(q[3]) + vv * three(q[6])
     u_all = col_coords(0.0, cols, cols)
-    spare = jnp.zeros((tall - rows - 2, EDGE), jnp.float32)
     for m in range(tiles):
         at = slice(m * EDGE, (m + 1) * EDGE)
         um = jnp.broadcast_to(u_all[:, at], (TILE, EDGE))
@@ -580,11 +595,7 @@
         for b in range(bases):
             factor = plane[b, 0:tall] + three(um * plane[b, tall : tall + TILE])
             model = model + factor * basis[b, m * tall : (m + 1) * tall]
-        science = jnp.concatenate([exp_ref[:, at], edge_recv[1, 0:1, at], spare, edge_recv[0, 0:1, at]], axis=0)
-        clean = jnp.concatenate(
-            [mask_ref[:, at].astype(jnp.float32), edge_recv[1, 1:2, at], spare, edge_recv[0, 1:2, at]], axis=0
-        )
-        diff[:, at] = clean * (science - model)
+        diff[:, at] = diff[:, at] - clean_ref[:, at] * model
 
     across.wait_send()
     for c in flying:
@@ -674,6 +685,7 @@
             pltpu.VMEM((bases, tiles * tall, EDGE), f32),
             pltpu.VMEM((fit, EDGE), f32),
             pltpu.VMEM((bases, tall + TILE, EDGE), f32),
+            pltpu.VMEM((tall, cols), f32),
             pltpu.VMEM((max(1, len(radices)), packed, EDGE), f32),
             pltpu.VMEM((slots, packed, EDGE), f32),
             pltpu.SemaphoreType.DMA((6,)),

time: 19.5 us -> 19.5 us (level)
  no operation moved by 1% of the time
where the time goes in v6:
time: 19.5 us; the launch traced here: 19.3 us
  Pallas kernels  18.7 us (96%)
  between operations  0.64 us (3%)
    pallas_call x1, Pallas kernels, shards(): pl.pallas_call(functools.partial(kernel, stripes, float(rows * stripes),...  17.9 us
    pallas_call x1, Pallas kernels, shards(): pl.pallas_call(finish_kernel, out_shape=(jax.ShapeDtypeStruct((rows, cols...  0.8 us

profile of v6, /device:TPU:0, one launch (start us, length us, event | category | flops | bytes accessed | tf_op | source)
XLA Modules:
  0.0 19.3 jit_solution(11485536468972345318)
XLA Ops:
  0.6 17.9 %fused.1 = (f32[24,2048]{1,0:T(8,128)S(1)}, f32[1,64]{1,0:T(1,128)S(1)}) custom-call(f32[16,1024]{1,0:T(8,128)} %tmpl_hbm.1, f32[16,2048]{1,0:T(8,128)} %bitcast.3, s32[16,2048]{1,0:T(8,128)} %bitcast.4, s32[1,16]{1,0:T(1,128)} %blk_hbm.1, f32[19,19]{1,0:T(8,128)} %rowf_hbm.1, f32[19,19]{1,0:T(8,128)} %colf_hbm.1), custom_call_target="tpu_custom_call" | custom-call | tf_op jit(solution)/shard_map/fused/pallas_call | solution.py:655
  18.5 0.8 %finish.1 = (f32[16,2048]{1,0:T(8,128)}, f32[1,64]{1,0:T(1,128)}) custom-call(f32[24,2048]{1,0:T(8,128)S(1)} %get-tuple-element.6.diff_ref, f32[1,64]{1,0:T(1,128)S(1)} %get-tuple-element.7.coef_ref), custom_call_target="tpu_custom_call" | custom-call | tf_op jit(solution)/shard_map/finish/pallas_call | solution.py:703

commit v7 on v6

--- a/solution.py
+++ b/solution.py
@@ -14,7 +14,7 @@
 BLOCK = 8
 REACH = HALF + 1
 VMEM_GRANT = 32 * 1024 * 1024
-GRAM_EARLY = 2
+GRAM_EARLY = 3
 MESH = pl.DeviceIdType.MESH
 LANE_DOT = (((1,), (1,)), ((), ()))
 

time: 19.5 us -> 19.5 us (level)
  no operation moved by 1% of the time
where the time goes in v7:
time: 19.5 us; the launch traced here: 19.4 us
  Pallas kernels  18.7 us (96%)
  between operations  0.64 us (3%)
    pallas_call x1, Pallas kernels, shards(): pl.pallas_call(functools.partial(kernel, stripes, float(rows * stripes),...  17.9 us
    pallas_call x1, Pallas kernels, shards(): pl.pallas_call(finish_kernel, out_shape=(jax.ShapeDtypeStruct((rows, cols...  0.8 us

profile of v7, /device:TPU:0, one launch (start us, length us, event | category | flops | bytes accessed | tf_op | source)
XLA Modules:
  0.0 19.4 jit_solution(16956488528569125139)
XLA Ops:
  0.6 17.9 %fused.1 = (f32[24,2048]{1,0:T(8,128)S(1)}, f32[1,64]{1,0:T(1,128)S(1)}) custom-call(f32[16,1024]{1,0:T(8,128)} %tmpl_hbm.1, f32[16,2048]{1,0:T(8,128)} %bitcast.3, s32[16,2048]{1,0:T(8,128)} %bitcast.4, s32[1,16]{1,0:T(1,128)} %blk_hbm.1, f32[19,19]{1,0:T(8,128)} %rowf_hbm.1, f32[19,19]{1,0:T(8,128)} %colf_hbm.1), custom_call_target="tpu_custom_call" | custom-call | tf_op jit(solution)/shard_map/fused/pallas_call | solution.py:655
  18.6 0.8 %finish.1 = (f32[16,2048]{1,0:T(8,128)}, f32[1,64]{1,0:T(1,128)}) custom-call(f32[24,2048]{1,0:T(8,128)S(1)} %get-tuple-element.6.diff_ref, f32[1,64]{1,0:T(1,128)S(1)} %get-tuple-element.7.coef_ref), custom_call_target="tpu_custom_call" | custom-call | tf_op jit(solution)/shard_map/finish/pallas_call | solution.py:703
